TPU v7x, 256 devices: a whole 4x4x8 slice. The times are simulated.
256 devices in a mesh: seq: 64 (over z, y, core), head: 4 (over x).
Axes of the slice: x: 4, y: 4, z: 8, core: 2. Of those that a mesh axis runs over, the one named last changes fastest.
Arguments:
- query_vectors: bfloat16 [131072, 1024], P('seq', 'head'), may hold values from -6 to 6
- key_vectors: bfloat16 [131072, 128], P('seq'), may hold values from -6 to 6
- value_vectors: bfloat16 [131072, 128], P('seq'), may hold values from -6 to 6
- output_grad: bfloat16 [131072, 1024], P('seq', 'head'), may hold values from -48 to 48
- random_blocks: int32 [1024, 3], P('seq'), may hold values from 0 to 1023, as said below
- global_blocks: int32 [2], replicated, may hold values from 0 to 1023
Outputs:
- query_grad: bfloat16 [131072, 1024], P('seq', 'head')
- key_grad: bfloat16 [131072, 128], P('seq')
- value_grad: bfloat16 [131072, 128], P('seq')
Inputs may be any that keep to these rules, and one draw needn't show every extreme that they name: `random_blocks`: take the query blocks in aligned runs of 16 and the key blocks in aligned runs of 16: all entries of one run of query blocks that fall into one run of key blocks name the same key block.
All inputs are finite; a program needn't handle non-finite values.
Results may differ from a plain program's by a relative error of at most 0.012.
Values may be sent and summed in bfloat16 or wider, within the bound.
A program may use at most 128 MiB of HBM per device.

v0:
```python
import jax
import jax.numpy as jnp
from jax import lax
from jax.sharding import PartitionSpec as P

DH = 128
BLOCK = 128
R = 3
G = 2


def with_halo(value, sides, width):
    for axis, dim in sides:
        size, length = (lax.axis_size(axis), value.shape[dim])
        up = [(i, (i + 1) % size) for i in range(size - 1)]
        down = [(j, i) for i, j in up]
        last = lax.slice_in_dim(value, length - width, length, axis=dim)
        first = lax.slice_in_dim(value, 0, width, axis=dim)
        before = lax.ppermute(last, axis, up)
        after = lax.ppermute(first, axis, down)
        value = jnp.concatenate([before, value, after], axis=dim)
    return value


def from_root(value, axis, source):
    kept = jnp.where(lax.axis_index(axis) == source, value, 0).astype(value.dtype)
    return lax.psum(kept, axis)


def from_behind(block, axis, distance):
    devices = range(lax.axis_size(axis))
    route = [(i - distance, i) for i in devices if i - distance in devices]
    return lax.ppermute(block, axis, route)


def softmax_rows(scores):
    largest = jnp.max(scores, axis=-1, keepdims=True)
    powers = jnp.exp(scores - largest)
    return powers / jnp.sum(powers, axis=-1, keepdims=True)


def body(query_vectors, key_vectors, value_vectors, output_grad, random_blocks, global_blocks):
    seq_count = lax.axis_size("seq")
    seq_index = lax.axis_index("seq")
    rows_dev = query_vectors.shape[0]
    blocks_dev = rows_dev // BLOCK
    heads_dev = query_vectors.shape[1] // DH
    factor = float(DH) ** (-0.5)
    pair_width = 2 * DH
    listed = 3 + R + G
    group_size = 4
    rounds = blocks_dev // group_size
    key_value = jnp.concatenate([key_vectors, value_vectors], axis=1)
    pair_blocks = key_value.reshape(blocks_dev, BLOCK, pair_width)
    owners = random_blocks // blocks_dev
    within = random_blocks % blocks_dev
    peer_ids = jnp.arange(seq_count, dtype=jnp.int32)
    matched = owners[:, :, None] == peer_ids[None, None, :]
    wanted = jnp.max(jnp.where(matched, within[:, :, None], -1), axis=(0, 1))
    requested = lax.all_to_all(
        wanted.reshape(seq_count, 1), "seq", split_axis=0, concat_axis=0, tiled=True
    )[:, 0]
    served = pair_blocks[jnp.clip(requested, 0, blocks_dev - 1)]
    fetched = lax.all_to_all(served, "seq", split_axis=0, concat_axis=0, tiled=True)
    extended = with_halo(key_value, (("seq", 0),), BLOCK)
    extended = extended.reshape(blocks_dev + 2, BLOCK, pair_width)
    global_list = []
    for global_slot in range(G):
        target = global_blocks[global_slot]
        fragment = lax.dynamic_index_in_dim(pair_blocks, target % blocks_dev, 0, keepdims=False)
        global_list.append(from_root(fragment, "seq", target // blocks_dev))
    global_pairs = jnp.stack(global_list)
    first_block = seq_index * blocks_dev
    total_blocks = seq_count * blocks_dev
    query_blocks = query_vectors.reshape(blocks_dev, BLOCK, heads_dev, DH)
    grad_blocks = output_grad.reshape(blocks_dev, BLOCK, heads_dev, DH)

    def advance(totals, position):
        window_acc, random_acc, global_acc = totals
        offset = position * group_size
        beside_all = lax.dynamic_slice_in_dim(extended, offset, group_size + 2, 0)
        window_panels = jnp.stack(
            [
                beside_all[0:group_size],
                beside_all[1 : group_size + 1],
                beside_all[2 : group_size + 2],
            ],
            axis=1,
        )
        owner_rows = lax.dynamic_slice_in_dim(owners, offset, group_size, 0)
        remote_panels = fetched[owner_rows]
        global_part = jnp.broadcast_to(global_pairs[None], (group_size, G, BLOCK, pair_width))
        panels = jnp.concatenate([window_panels, remote_panels, global_part], axis=1)
        panels = panels.reshape(group_size, listed * BLOCK, pair_width)
        key_row_matrix = panels[:, :, :DH]
        value_row_matrix = panels[:, :, DH:]
        query_row_matrix = lax.dynamic_slice_in_dim(query_blocks, offset, group_size, 0)
        gradient_rows = lax.dynamic_slice_in_dim(grad_blocks, offset, group_size, 0)
        block_ids = first_block + offset + jnp.arange(group_size, dtype=jnp.int32)
        allowed = jnp.concatenate(
            [
                (block_ids > 0)[:, None],
                jnp.ones((group_size, 1), dtype=jnp.bool_),
                (block_ids < total_blocks - 1)[:, None],
                jnp.ones((group_size, R + G), dtype=jnp.bool_),
            ],
            axis=1,
        )
        visible = jnp.repeat(allowed, BLOCK, axis=1)
        scores = (
            jnp.einsum(
                "awst,axt->aswx",
                query_row_matrix,
                key_row_matrix,
                preferred_element_type=jnp.float32,
            )
            * factor
        )
        scores = jnp.where(visible[:, None, None, :], scores, -jnp.inf)
        attention = softmax_rows(scores)
        attention_reduced = attention.astype(jnp.bfloat16)
        outputs = jnp.einsum(
            "uwsn,unj->uswj",
            attention_reduced,
            value_row_matrix,
            preferred_element_type=jnp.float32,
        )
        row_delta = jnp.sum(gradient_rows.astype(jnp.float32) * outputs, axis=-1)
        prob_grad = jnp.einsum(
            "awst,axt->aswx", gradient_rows, value_row_matrix, preferred_element_type=jnp.float32
        )
        score_gradient = (
            attention * (prob_grad - jnp.transpose(row_delta, (0, 2, 1))[..., None])
        ).astype(jnp.bfloat16)
        query_part = (
            jnp.einsum(
                "uwsn,unj->uswj", score_gradient, key_row_matrix, preferred_element_type=jnp.float32
            )
            * factor
        ).astype(jnp.bfloat16)
        key_part = (
            jnp.einsum(
                "uwva,uvwp->uap",
                score_gradient,
                query_row_matrix,
                preferred_element_type=jnp.float32,
            )
            * factor
        )
        value_part = jnp.einsum(
            "uwva,uvwp->uap", attention_reduced, gradient_rows, preferred_element_type=jnp.float32
        )
        gradients = jnp.concatenate([key_part, value_part], axis=-1).reshape(
            group_size, listed, BLOCK, pair_width
        )
        spread = jnp.zeros((group_size + 2, BLOCK, pair_width), dtype=jnp.float32)
        spread = spread.at[0:group_size].add(gradients[:, 0])
        spread = spread.at[1 : group_size + 1].add(gradients[:, 1])
        spread = spread.at[2 : group_size + 2].add(gradients[:, 2])
        updated = lax.dynamic_slice_in_dim(window_acc, offset, group_size + 2, 0) + spread
        window_acc = lax.dynamic_update_slice_in_dim(window_acc, updated, offset, 0)
        onehot = (owner_rows[:, :, None] == peer_ids[None, None, :]).astype(jnp.float32)
        random_acc = random_acc + jnp.einsum(
            "brn,brxc->nxc", onehot, gradients[:, 3 : 3 + R], precision=lax.Precision.HIGHEST
        )
        global_acc = global_acc + jnp.sum(gradients[:, 3 + R :], axis=0)
        return (
            (window_acc, random_acc, global_acc),
            query_part.reshape(group_size, BLOCK, heads_dev * DH),
        )

    start_totals = (
        jnp.zeros((blocks_dev + 2, BLOCK, pair_width), dtype=jnp.float32),
        jnp.zeros((seq_count, BLOCK, pair_width), dtype=jnp.float32),
        jnp.zeros((G, BLOCK, pair_width), dtype=jnp.float32),
    )
    (window_acc, random_acc, global_acc), query_parts = lax.scan(
        advance, start_totals, jnp.arange(rounds, dtype=jnp.int32)
    )
    query_grad = query_parts.reshape(rows_dev, heads_dev * DH)
    into_last = from_behind(window_acc[0].astype(jnp.bfloat16), "seq", -1).astype(jnp.float32)
    into_first = from_behind(window_acc[blocks_dev + 1].astype(jnp.bfloat16), "seq", 1).astype(
        jnp.float32
    )
    local_sum = window_acc[1 : blocks_dev + 1]
    local_sum = local_sum.at[blocks_dev - 1].add(into_last)
    local_sum = local_sum.at[0].add(into_first)
    global_total_sum = lax.psum(global_acc, "seq")
    block_range = jnp.arange(blocks_dev, dtype=jnp.int32)
    owned_indicator = (
        (global_blocks[None, :] // blocks_dev == seq_index)
        & (global_blocks[None, :] % blocks_dev == block_range[:, None])
    ).astype(jnp.float32)
    local_sum = local_sum + jnp.einsum(
        "ar,rdi->adi", owned_indicator, global_total_sum, precision=lax.Precision.HIGHEST
    )
    served_hot = (requested[None, :] == block_range[:, None]).astype(jnp.float32)
    returned = lax.all_to_all(
        random_acc.astype(jnp.bfloat16), "seq", split_axis=0, concat_axis=0, tiled=True
    ).astype(random_acc.dtype)
    local_sum = local_sum + jnp.einsum(
        "je,exc->jxc", served_hot, returned, precision=lax.Precision.HIGHEST
    )
    finished = lax.psum(local_sum.astype(jnp.bfloat16), "head")
    finished = finished.reshape(rows_dev, pair_width)
    return (query_grad, finished[:, :DH], finished[:, DH:])


def solution(mesh):
    return jax.shard_map(
        body,
        mesh=mesh,
        in_specs=(
            P("seq", "head"),
            P("seq", None),
            P("seq", None),
            P("seq", "head"),
            P("seq", None),
            P(),
        ),
        out_specs=(P("seq", "head"), P("seq", None), P("seq", None)),
        check_vma=False,
    )
```

profile of v0, /device:TPU:8, one launch (start us, length us, event | category | flops | bytes accessed | tf_op | source)
XLA Modules:
  0.0 700.6 jit_solution(18152049485967785271)
XLA Ops:
  8.9 12.1 %all-to-all-start = ((s32[64,1,1]{2,1,0:T(1,128)}), s32[64,1,1]{2,1,0:T(1,128)S(1)}, u32[]{:S(2)}, u32[]{:S(2)}) async-start(s32[64,1,1]{2,1,0:T(1,128)} %copy.161), calls=%async_computation | async-start | bytes 65536 | tf_op jit(solution)/shard_map/all_to_all | solution.py:60
  23.3 6.2 all-to-all-done
  29.6 2.8 fusion.47
  32.4 2.7 gather_fusion.1
  35.1 6.6 all-to-all-start.1
  48.3 2.0 collective-permute-start
  50.4 3.5 collective-permute-start.1
  56.2 178.6 %all-reduce.10.cloned.1.call-done = (bf16[1,128,256]{2,1,0:T(8,128)(2,1)}, bf16[1,128,256]{2,1,0:T(8,128)(2,1)}) async-done(((bf16[1,128,256]{2,1,0:T(8,128)(2,1)}, bf16[1,128,256]{2,1,0:T(8,128)(2,1)}), (bf16[1,128,256]{2,1,0:T(8,128)(2,1)}, bf16[1,128,256]{2,1,0:T(8,128)(2,1)})) %all-reduce.10.cloned.1.call-update) | async-done | bytes 131088 | tf_op jit(solution)/shard_map/psum | solution.py:27
  238.5 181.6 %while.25 = (s32[]{:T(128)}, f32[18,128,256]{1,2,0:T(8,128)}, f32[64,128,256]{2,0,1:T(8,128)}, f32[2,128,256]{1,0,2:T(2,128)}, bf16[4,4,128,256]{3,2,1,0:T(8,128...) while((s32[]{:T(128)}, f32[18,128,256]{1,2,0:T(8,128)}, ...), condition=%wide.region_8.9_spmd.clone, body=%wide.region_3.8_spmd.clone.sunk | while | flops 1932396416 | bytes 146449488 | solution.py:177
  241.7 2.8 gather_fusion
  248.3 1.9 fusion.96
  255.1 2.9 copy.238
  258.2 2.9 slice_reduce_fusion.2
  262.7 6.8 fusion.100
  274.5 6.3 bitcast_add_fusion.2
  284.0 2.8 gather_fusion
  290.6 1.9 fusion.96
  297.4 2.9 copy.238
  300.4 2.9 slice_reduce_fusion.2
  303.4 2.0 select_add_fusion.2
  306.1 6.8 fusion.100
  317.9 9.3 %bitcast_add_fusion.2 = f32[64,128,256]{2,0,1:T(8,128)} fusion(f32[64,128,256]{2,0,1:T(8,128)} %get-tuple-element.561, pred[]{:T(512)S(6)} %compare.58, f32[4,3,128,256]{3,0,1,2:T(4,128)S(1)} %copy-done.1, s32[4,3]{0,1:T(4,128)S(1)} %copy.240), kind=kOutput, calls=%fused_computation.4.clone.1 | convolution fusion | flops 306184960 | bytes 18350128 | tf_op jit(solution)/shard_map/while/body/eval_jaxpr/brn,brxc->nxc/dot_general | solution.py:163
  330.4 2.8 gather_fusion
  343.8 2.9 copy.238
  346.9 2.9 slice_reduce_fusion.2
  349.8 2.0 select_add_fusion.2
  352.5 6.8 fusion.100
  364.4 9.3 %bitcast_add_fusion.2 = f32[64,128,256]{2,0,1:T(8,128)} fusion(f32[64,128,256]{2,0,1:T(8,128)} %get-tuple-element.561, pred[]{:T(512)S(6)} %compare.58, f32[4,3,128,256]{3,0,1,2:T(4,128)S(1)} %copy-done.1, s32[4,3]{0,1:T(4,128)S(1)} %copy.240), kind=kOutput, calls=%fused_computation.4.clone.1 | convolution fusion | flops 306184960 | bytes 18350128 | tf_op jit(solution)/shard_map/while/body/eval_jaxpr/brn,brxc->nxc/dot_general | solution.py:163
  376.9 2.8 gather_fusion
  390.2 2.9 copy.238
  393.3 2.9 slice_reduce_fusion.2
  396.3 2.0 select_add_fusion.2
  399.0 6.8 fusion.100
  410.8 9.3 %bitcast_add_fusion.2 = f32[64,128,256]{2,0,1:T(8,128)} fusion(f32[64,128,256]{2,0,1:T(8,128)} %get-tuple-element.561, pred[]{:T(512)S(6)} %compare.58, f32[4,3,128,256]{3,0,1,2:T(4,128)S(1)} %copy-done.1, s32[4,3]{0,1:T(4,128)S(1)} %copy.240), kind=kOutput, calls=%fused_computation.4.clone.1 | convolution fusion | flops 306184960 | bytes 18350128 | tf_op jit(solution)/shard_map/while/body/eval_jaxpr/brn,brxc->nxc/dot_general | solution.py:163
  420.1 9.8 %copy.220 = bf16[64,128,256]{2,1,0:T(8,128)(2,1)} copy(f32[64,128,256]{2,0,1:T(8,128)} %get-tuple-element.285) | data formatting | bytes 12582912 | tf_op jit(solution)/shard_map/while | solution.py:177
  429.9 8.4 %all-to-all-start.2 = ((bf16[64,128,256]{2,1,0:T(8,128)(2,1)}), bf16[64,128,256]{2,1,0:T(8,128)(2,1)}, u32[]{:S(2)}, u32[]{:S(2)}) async-start(bf16[64,128,256]{2,1,0:T(8,128)(2,1)} %copy.220), calls=%async_computation.2 | async-start | bytes 8388608 | tf_op jit(solution)/shard_map/all_to_all | solution.py:198
  438.4 2.0 copy.168
  442.2 2.0 collective-permute-start.2
  444.2 2.3 copy.167
  448.4 2.2 slice.256
  450.6 2.3 collective-permute-start.3
  454.0 2.0 scatter-add.19
  458.9 76.0 %all-to-all-done.2 = bf16[64,128,256]{2,1,0:T(8,128)(2,1)} async-done(((bf16[64,128,256]{2,1,0:T(8,128)(2,1)}), bf16[64,128,256]{2,1,0:T(8,128)(2,1)}, u32[]{:S(2)}, u32[]{:S(2)}) %all-to-all-start.2) | async-done | bytes 4194336 | tf_op jit(solution)/shard_map/all_to_all | solution.py:198
  534.9 5.9 fusion.32
  540.8 97.0 %all-reduce.6.cloned.1.call-done = f32[2,128,256]{2,0,1:T(2,128)} async-done(((f32[2,128,256]{2,0,1:T(2,128)}), f32[2,128,256]{2,0,1:T(2,128)}) %all-reduce.6.cloned.1.call-update) | async-done | bytes 262160 | tf_op jit(solution)/shard_map/psum | solution.py:188
  637.7 2.9 add_convert_fusion
  642.0 49.8 %all-reduce.8.cloned.1.call-done = bf16[2048,256]{1,0:T(8,128)(2,1)} async-done(((bf16[2048,256]{1,0:T(8,128)(2,1)}), bf16[2048,256]{1,0:T(8,128)(2,1)}) %all-reduce.8.cloned.1.call-update) | async-done | bytes 1048592 | tf_op jit(solution)/shard_map/psum | solution.py:204
  691.8 2.2 fusion.50
  (227 shorter events, 92.8 us)
Async XLA Ops:
  8.9 20.7 %all-to-all-start = ((s32[64,1,1]{2,1,0:T(1,128)}), s32[64,1,1]{2,1,0:T(1,128)S(1)}, u32[]{:S(2)}, u32[]{:S(2)}) async-start(s32[64,1,1]{2,1,0:T(1,128)} %copy.161), calls=%async_computation | async-start | bytes 65536 | tf_op jit(solution)/shard_map/all_to_all | solution.py:60
  35.1 6.7 copy-start.8
  35.1 18.8 %copy-start.5 = (bf16[2048,256]{1,0:T(8,128)(2,1)S(1)}, bf16[2048,256]{1,0:T(8,128)(2,1)}, u32[]{:S(2)}) copy-start(bf16[2048,256]{1,0:T(8,128)(2,1)} %param.18) | copy-start | bytes 3145732
  35.1 201.7 %all-to-all-start.1 = ((bf16[64,128,256]{2,1,0:T(8,128)(2,1)}), bf16[64,128,256]{2,1,0:T(8,128)(2,1)}, u32[]{:S(2)}, u32[]{:S(2)}) async-start(bf16[64,128,256]{2,1,0:T(8,128)(2,1)} %gather_fusion.1), calls=%async_computation.1 | async-start | bytes 8388608 | tf_op jit(solution)/shard_map/all_to_all | solution.py:64
  41.7 13.3 %copy-start.6 = (bf16[2048,256]{1,0:T(8,128)(2,1)S(1)}, bf16[2048,256]{1,0:T(8,128)(2,1)}, u32[]{:S(2)}) copy-start(bf16[2048,256]{1,0:T(8,128)(2,1)} %param.21) | copy-start | bytes 3145732
  41.8 193.1 %all-reduce.10.cloned.1.call-start = ((), (), s32[]{:S(2)}) async-start(), calls=%async_computation.5 | async-start | bytes 262144 | tf_op jit(solution)/shard_map/psum | solution.py:27
  48.3 187.4 %collective-permute-start = (bf16[128,256]{1,0:T(8,128)(2,1)S(1)}, bf16[128,256]{1,0:T(8,128)(2,1)S(1)}, u32[]{:S(2)}, u32[]{:S(2)}) collective-permute-start(bf16[128,256]{1,0:T(8,128)(2,1)S(1)} %get-tuple-element.429), channel_id=1, source_target_pairs={{0,4},{4,8},{8,12},{12,16},{16,20},{20,24},{24,28},{28,32},{32,36}... | collective-permute-start | bytes 196616 | tf_op jit(solution)/shard_map/ppermute | solution.py:19
  50.4 185.3 %collective-permute-start.1 = (bf16[128,256]{1,0:T(8,128)(2,1)S(1)}, bf16[128,256]{1,0:T(8,128)(2,1)S(1)}, u32[]{:S(2)}, u32[]{:S(2)}) collective-permute-start(bf16[128,256]{1,0:T(8,128)(2,1)S(1)} %get-tuple-element.430), channel_id=1, source_target_pairs={{4,0},{8,4},{12,8},{16,12},{20,16},{24,20},{28,24},{32,28},{36,32}... | collective-permute-start | bytes 196616 | tf_op jit(solution)/shard_map/ppermute | solution.py:20
  261.1 8.4 %copy-start = (f32[128,8,8,128]{3,2,1,0:T(8,128)S(1)}, f32[128,8,8,128]{3,2,1,0:T(8,128)}, u32[]{:S(2)}) copy-start(f32[128,8,8,128]{3,2,1,0:T(8,128)} %copy.238) | copy-start | bytes 12582916 | tf_op jit(solution)/shard_map/while
  271.7 1.8 copy-start.2
  273.0 1.5 copy-start.1
  274.5 6.3 copy-start.3
  303.4 9.5 %copy-start = (f32[128,8,8,128]{3,2,1,0:T(8,128)S(1)}, f32[128,8,8,128]{3,2,1,0:T(8,128)}, u32[]{:S(2)}) copy-start(f32[128,8,8,128]{3,2,1,0:T(8,128)} %copy.238) | copy-start | bytes 12582916 | tf_op jit(solution)/shard_map/while
  315.0 1.8 copy-start.2
  316.4 1.5 copy-start.1
  317.9 9.3 %copy-start.3 = (f32[18,128,256]{1,2,0:T(8,128)}, f32[18,128,256]{1,2,0:T(8,128)S(1)}, u32[]{:S(2)}) copy-start(f32[18,128,256]{1,2,0:T(8,128)S(1)} %add_dynamic-update-slice_fusion.5) | copy-start | bytes 7077892 | tf_op jit(solution)/shard_map/while
  349.8 9.5 %copy-start = (f32[128,8,8,128]{3,2,1,0:T(8,128)S(1)}, f32[128,8,8,128]{3,2,1,0:T(8,128)}, u32[]{:S(2)}) copy-start(f32[128,8,8,128]{3,2,1,0:T(8,128)} %copy.238) | copy-start | bytes 12582916 | tf_op jit(solution)/shard_map/while
  361.5 1.8 copy-start.2
  362.8 1.5 copy-start.1
  364.4 9.3 %copy-start.3 = (f32[18,128,256]{1,2,0:T(8,128)}, f32[18,128,256]{1,2,0:T(8,128)S(1)}, u32[]{:S(2)}) copy-start(f32[18,128,256]{1,2,0:T(8,128)S(1)} %add_dynamic-update-slice_fusion.5) | copy-start | bytes 7077892 | tf_op jit(solution)/shard_map/while
  396.3 9.5 %copy-start = (f32[128,8,8,128]{3,2,1,0:T(8,128)S(1)}, f32[128,8,8,128]{3,2,1,0:T(8,128)}, u32[]{:S(2)}) copy-start(f32[128,8,8,128]{3,2,1,0:T(8,128)} %copy.238) | copy-start | bytes 12582916 | tf_op jit(solution)/shard_map/while
  407.9 1.8 copy-start.2
  409.3 1.5 copy-start.1
  410.8 9.3 %copy-start.3 = (f32[18,128,256]{1,2,0:T(8,128)}, f32[18,128,256]{1,2,0:T(8,128)S(1)}, u32[]{:S(2)}) copy-start(f32[18,128,256]{1,2,0:T(8,128)S(1)} %add_dynamic-update-slice_fusion.5) | copy-start | bytes 7077892 | tf_op jit(solution)/shard_map/while
  429.9 8.4 %copy-start.9 = (s32[2]{0:T(128)S(1)}, s32[2]{0:T(128)}, u32[]{:S(2)}) copy-start(s32[2]{0:T(128)} %param.23) | copy-start | bytes 28
  429.9 8.4 %copy-start.4 = (f32[18,128,256]{1,2,0:T(8,128)S(1)}, f32[18,128,256]{1,2,0:T(8,128)}, u32[]{:S(2)}) copy-start(f32[18,128,256]{1,2,0:T(8,128)} %get-tuple-element.283) | copy-start | bytes 7077892
  429.9 105.0 %all-to-all-start.2 = ((bf16[64,128,256]{2,1,0:T(8,128)(2,1)}), bf16[64,128,256]{2,1,0:T(8,128)(2,1)}, u32[]{:S(2)}, u32[]{:S(2)}) async-start(bf16[64,128,256]{2,1,0:T(8,128)(2,1)} %copy.220), calls=%async_computation.2 | async-start | bytes 8388608 | tf_op jit(solution)/shard_map/all_to_all | solution.py:198
  438.3 199.4 %all-reduce.6.cloned.1.call-start = ((), (), s32[]{:S(2)}) async-start(), calls=%async_computation.3 | async-start | bytes 524288 | tf_op jit(solution)/shard_map/psum | solution.py:188
  442.2 10.8 %collective-permute-start.2 = (bf16[128,256]{1,0:T(8,128)(2,1)S(1)}, bf16[128,256]{1,0:T(8,128)(2,1)S(1)}, u32[]{:S(2)}, u32[]{:S(2)}) collective-permute-start(bf16[128,256]{1,0:T(8,128)(2,1)S(1)} %get-tuple-element.424), channel_id=1, source_target_pairs={{4,0},{8,4},{12,8},{16,12},{20,16},{24,20},{28,24},{32,28},{36,32}... | collective-permute-start | bytes 196616 | tf_op jit(solution)/shard_map/ppermute | solution.py:33
  448.3 86.5 %copy-start.7 = (s32[64]{0:T(128)S(1)}, s32[64]{0:T(128)}, u32[]{:S(2)}) copy-start(s32[64]{0:T(128)} %get-tuple-element.382) | copy-start | bytes 772
  448.3 243.5 %all-reduce.8.cloned.1.call-start = ((), (), s32[]{:S(2)}) async-start(), calls=%async_computation.4 | async-start | bytes 2097152 | tf_op jit(solution)/shard_map/psum | solution.py:204
  450.6 6.3 collective-permute-start.3
Sparse Core Ops, SparseCore 0:
  48.4 186.3 all-reduce.9
  448.4 189.2 all-reduce.5
  642.2 49.6 all-reduce.7
where the time goes:
time: 702 us; the launch traced here: 701 us
  waiting for transfers between devices  409 us (58%)
  local copies, waits for them, and re-layouts  131 us (19%)
  matrix products  61.8 us (9%)
  other arithmetic  40.1 us (6%)
  starting transfers between devices  37.1 us (5%)
  between operations  19.2 us (3%)
    psum x1, waiting for transfers between devices, from_root(): return lax.psum(kept, axis)  179 us
    psum x1, waiting for transfers between devices, body(): global_total_sum = lax.psum(global_acc, 'seq')  97 us
    all_to_all x1, waiting for transfers between devices, body(): lax.all_to_all(random_acc.astype(jnp.bfloat16), 'seq', split_axis=0, conc...  76 us
    psum x1, waiting for transfers between devices, body(): finished = lax.psum(local_sum.astype(jnp.bfloat16), 'head')  49.8 us
    while x64, local copies, waits for them, and re-layouts  35.7 us
    dot_general x4, matrix products, advance(): jnp.einsum('brn,brxc->nxc', onehot, gradients[:, 3:3 + R], precision=lax....  34.2 us
    slice x4, local copies, waits for them, and re-layouts, advance(): spread = spread.at[2:group_size + 2].add(gradients[:, 2])  27.3 us
    while x4, local copies, waits for them, and re-layouts, body(): lax.scan(advance, start_totals, jnp.arange(rounds, dtype=jnp.int32))  15.9 us
  transfers between devices with their start and end apart: 10, of which 6 were waited for; matrix products, arithmetic and copies ran while one was open for 4% of the time, Pallas kernels for 0%

commit v1 on v0

--- a/solution.py
+++ b/solution.py
@@ -185,7 +185,7 @@
     local_sum = window_acc[1 : blocks_dev + 1]
     local_sum = local_sum.at[blocks_dev - 1].add(into_last)
     local_sum = local_sum.at[0].add(into_first)
-    global_total_sum = lax.psum(global_acc, "seq")
+    global_total_sum = jnp.sum(lax.all_gather(global_acc, "seq"), axis=0)
     block_range = jnp.arange(blocks_dev, dtype=jnp.int32)
     owned_indicator = (
         (global_blocks[None, :] // blocks_dev == seq_index)

time: 702 us -> 655 us (0.933)
  waiting for transfers between devices: 409 us -> 353 us
    psum x1 -> x0, waiting for transfers between devices: 97 us -> none  [body(): global_total_sum = lax.psum(global_acc, 'seq')]
    all_to_all x1, waiting for transfers between devices: 76 us -> 110 us  [body(): lax.all_to_all(random_acc.astype(jnp.bfloat16), 'seq', split_axis=0, conc...]
    all_gather x0 -> x1, waiting for transfers between devices: none -> 7.53 us  [body(): global_total_sum = jnp.sum(lax.all_gather(global_acc, 'seq'), axis=0)]
  transfers between devices with their start and end apart: 10 -> 10, of which waited for: 6 -> 6; matrix products, arithmetic and copies ran while one was open for 4% -> 6% of each run, Pallas kernels for 0% -> 0%
where the time goes in v1:
time: 655 us; the launch traced here: 653 us
  waiting for transfers between devices  353 us (54%)
  local copies, waits for them, and re-layouts  131 us (20%)
  matrix products  61.8 us (9%)
  other arithmetic  46.9 us (7%)
  starting transfers between devices  37.1 us (6%)
  between operations  19.2 us (3%)
    psum x1, waiting for transfers between devices, from_root(): return lax.psum(kept, axis)  179 us
    all_to_all x1, waiting for transfers between devices, body(): lax.all_to_all(random_acc.astype(jnp.bfloat16), 'seq', split_axis=0, conc...  110 us
    psum x1, waiting for transfers between devices, body(): finished = lax.psum(local_sum.astype(jnp.bfloat16), 'head')  50.8 us
    while x64, local copies, waits for them, and re-layouts  35.9 us
    dot_general x4, matrix products, advance(): jnp.einsum('brn,brxc->nxc', onehot, gradients[:, 3:3 + R], precision=lax....  34.3 us
    slice x4, local copies, waits for them, and re-layouts, advance(): spread = spread.at[2:group_size + 2].add(gradients[:, 2])  27.7 us
    while x4, local copies, waits for them, and re-layouts, body(): lax.scan(advance, start_totals, jnp.arange(rounds, dtype=jnp.int32))  15.9 us
  transfers between devices with their start and end apart: 10, of which 6 were waited for; matrix products, arithmetic and copies ran while one was open for 6% of the time, Pallas kernels for 0%

profile of v1, /device:TPU:8, one launch (start us, length us, event | category | flops | bytes accessed | tf_op | source)
XLA Modules:
  0.0 652.9 jit_solution(9095257188172763972)
XLA Ops:
  8.9 12.1 %all-to-all-start = ((s32[64,1,1]{2,1,0:T(1,128)}), s32[64,1,1]{2,1,0:T(1,128)S(1)}, u32[]{:S(2)}, u32[]{:S(2)}) async-start(s32[64,1,1]{2,1,0:T(1,128)} %copy.161), calls=%async_computation | async-start | bytes 65536 | tf_op jit(solution)/shard_map/all_to_all | solution.py:60
  23.3 6.2 all-to-all-done
  29.6 2.8 fusion.48
  32.4 2.8 gather_fusion.1
  35.2 6.6 %all-to-all-start.1 = ((bf16[64,128,256]{2,1,0:T(8,128)(2,1)}), bf16[64,128,256]{2,1,0:T(8,128)(2,1)}, u32[]{:S(2)}, u32[]{:S(2)}) async-start(bf16[64,128,256]{2,1,0:T(8,128)(2,1)} %gather_fusion.1), calls=%async_computation.1 | async-start | bytes 8388608 | tf_op jit(solution)/shard_map/all_to_all | solution.py:64
  48.4 2.0 collective-permute-start
  50.5 3.5 collective-permute-start.1
  56.4 178.5 %all-reduce.7.cloned.1.call-done = (bf16[1,128,256]{2,1,0:T(8,128)(2,1)}, bf16[1,128,256]{2,1,0:T(8,128)(2,1)}) async-done(((bf16[1,128,256]{2,1,0:T(8,128)(2,1)}, bf16[1,128,256]{2,1,0:T(8,128)(2,1)}), (bf16[1,128,256]{2,1,0:T(8,128)(2,1)}, bf16[1,128,256]{2,1,0:T(8,128)(2,1)})) %all-reduce.7.cloned.1.call-update) | async-done | bytes 131088 | tf_op jit(solution)/shard_map/psum | solution.py:27
  238.5 182.2 %while.25 = (s32[]{:T(128)}, f32[18,128,256]{1,2,0:T(8,128)}, f32[64,128,256]{2,0,1:T(8,128)}, f32[2,128,256]{1,0,2:T(2,128)}, bf16[4,4,128,256]{3,2,1,0:T(8,128...) while((s32[]{:T(128)}, f32[18,128,256]{1,2,0:T(8,128)}, ...), condition=%wide.region_8.9_spmd.clone, body=%wide.region_3.8_spmd.clone.sunk | while | flops 1932396416 | bytes 146449488 | solution.py:177
  241.7 2.8 gather_fusion
  248.2 1.9 fusion.96
  255.0 3.0 copy.241
  258.2 2.9 slice_reduce_fusion.2
  262.7 6.9 %fusion.100 = (f32[4,1,128,256]{2,1,3,0:T(1,128)S(1)}, f32[4,1,128,256]{2,1,3,0:T(1,128)S(1)}, f32[4,1,128,256]{2,1,3,0:T(1,128)}) fusion(f32[4,8,128,256]{2,1,3,0:T(8,128)} %bitcast.194), kind=kLoop, calls=%fused_computation.109.clone.1 | loop fusion | bytes 3145728 | tf_op jit(solution)/shard_map/while/body/eval_jaxpr/slice | solution.py:159
  274.7 6.3 bitcast_add_fusion.2
  284.1 2.8 gather_fusion
  297.5 3.0 copy.241
  300.6 2.9 slice_reduce_fusion.2
  303.6 2.0 select_add_fusion.2
  306.3 6.9 %fusion.100 = (f32[4,1,128,256]{2,1,3,0:T(1,128)S(1)}, f32[4,1,128,256]{2,1,3,0:T(1,128)S(1)}, f32[4,1,128,256]{2,1,3,0:T(1,128)}) fusion(f32[4,8,128,256]{2,1,3,0:T(8,128)} %bitcast.194), kind=kLoop, calls=%fused_computation.109.clone.1 | loop fusion | bytes 3145728 | tf_op jit(solution)/shard_map/while/body/eval_jaxpr/slice | solution.py:159
  318.2 9.3 %bitcast_add_fusion.2 = f32[64,128,256]{2,0,1:T(8,128)} fusion(f32[64,128,256]{2,0,1:T(8,128)} %get-tuple-element.561, pred[]{:T(512)S(6)} %compare.58, f32[4,3,128,256]{3,0,1,2:T(4,128)S(1)} %copy-done.1, s32[4,3]{0,1:T(4,128)S(1)} %copy.243), kind=kOutput, calls=%fused_computation.4.clone.1 | convolution fusion | flops 306184960 | bytes 18350128 | tf_op jit(solution)/shard_map/while/body/eval_jaxpr/brn,brxc->nxc/dot_general | solution.py:163
  330.7 2.8 gather_fusion
  344.1 3.0 copy.241
  347.2 2.9 slice_reduce_fusion.2
  350.2 2.0 select_add_fusion.2
  352.9 6.9 %fusion.100 = (f32[4,1,128,256]{2,1,3,0:T(1,128)S(1)}, f32[4,1,128,256]{2,1,3,0:T(1,128)S(1)}, f32[4,1,128,256]{2,1,3,0:T(1,128)}) fusion(f32[4,8,128,256]{2,1,3,0:T(8,128)} %bitcast.194), kind=kLoop, calls=%fused_computation.109.clone.1 | loop fusion | bytes 3145728 | tf_op jit(solution)/shard_map/while/body/eval_jaxpr/slice | solution.py:159
  364.8 9.3 %bitcast_add_fusion.2 = f32[64,128,256]{2,0,1:T(8,128)} fusion(f32[64,128,256]{2,0,1:T(8,128)} %get-tuple-element.561, pred[]{:T(512)S(6)} %compare.58, f32[4,3,128,256]{3,0,1,2:T(4,128)S(1)} %copy-done.1, s32[4,3]{0,1:T(4,128)S(1)} %copy.243), kind=kOutput, calls=%fused_computation.4.clone.1 | convolution fusion | flops 306184960 | bytes 18350128 | tf_op jit(solution)/shard_map/while/body/eval_jaxpr/brn,brxc->nxc/dot_general | solution.py:163
  377.3 2.8 gather_fusion
  390.7 3.0 copy.241
  393.8 2.9 slice_reduce_fusion.2
  396.8 2.0 select_add_fusion.2
  399.5 6.9 %fusion.100 = (f32[4,1,128,256]{2,1,3,0:T(1,128)S(1)}, f32[4,1,128,256]{2,1,3,0:T(1,128)S(1)}, f32[4,1,128,256]{2,1,3,0:T(1,128)}) fusion(f32[4,8,128,256]{2,1,3,0:T(8,128)} %bitcast.194), kind=kLoop, calls=%fused_computation.109.clone.1 | loop fusion | bytes 3145728 | tf_op jit(solution)/shard_map/while/body/eval_jaxpr/slice | solution.py:159
  411.4 9.3 %bitcast_add_fusion.2 = f32[64,128,256]{2,0,1:T(8,128)} fusion(f32[64,128,256]{2,0,1:T(8,128)} %get-tuple-element.561, pred[]{:T(512)S(6)} %compare.58, f32[4,3,128,256]{3,0,1,2:T(4,128)S(1)} %copy-done.1, s32[4,3]{0,1:T(4,128)S(1)} %copy.243), kind=kOutput, calls=%fused_computation.4.clone.1 | convolution fusion | flops 306184960 | bytes 18350128 | tf_op jit(solution)/shard_map/while/body/eval_jaxpr/brn,brxc->nxc/dot_general | solution.py:163
  422.5 9.8 %copy.223 = bf16[64,128,256]{2,1,0:T(8,128)(2,1)} copy(f32[64,128,256]{2,0,1:T(8,128)} %get-tuple-element.285) | data formatting | bytes 12582912 | tf_op jit(solution)/shard_map/while | solution.py:177
  432.3 8.4 %all-to-all-start.2 = ((bf16[64,128,256]{2,1,0:T(8,128)(2,1)}), bf16[64,128,256]{2,1,0:T(8,128)(2,1)}, u32[]{:S(2)}, u32[]{:S(2)}) async-start(bf16[64,128,256]{2,1,0:T(8,128)(2,1)} %copy.223), calls=%async_computation.2 | async-start | bytes 8388608 | tf_op jit(solution)/shard_map/all_to_all | solution.py:198
  440.8 2.0 copy.168
  444.6 2.0 collective-permute-start.2
  446.7 2.4 copy.167
  449.0 2.3 slice.256
  451.3 2.3 collective-permute-start.3
  454.7 2.0 scatter-add.19
  459.2 109.6 %all-to-all-done.2 = bf16[64,128,256]{2,1,0:T(8,128)(2,1)} async-done(((bf16[64,128,256]{2,1,0:T(8,128)(2,1)}), bf16[64,128,256]{2,1,0:T(8,128)(2,1)}, u32[]{:S(2)}, u32[]{:S(2)}) %all-to-all-start.2) | async-done | bytes 4194336 | tf_op jit(solution)/shard_map/all_to_all | solution.py:198
  568.8 6.0 fusion.32
  574.8 7.5 %all-gather.3.cloned.1.call-done = f32[128,128,256]{2,1,0:T(8,128)} async-done(((f32[2,128,256]{2,1,0:T(8,128)}), f32[128,128,256]{2,1,0:T(8,128)}) %all-gather.3.cloned.1.call-update) | async-done | bytes 16777232 | tf_op jit(solution)/shard_map/all_gather | solution.py:188
  582.3 6.9 %reduce_sum.48 = f32[2,128,256]{2,1,0:T(8,128)S(1)} reduce(f32[64,2,128,256]{3,2,1,0:T(8,128)} %bitcast.207, f32[]{:T(128)} %constant.320.clone.1), dimensions={0}, to_apply=%region_9.10 | reduce | flops 4128768 | bytes 17039364 | tf_op jit(solution)/shard_map/reduce_sum | solution.py:188
  589.2 2.8 add_convert_fusion
  593.4 50.8 %all-reduce.5.cloned.1.call-done = bf16[2048,256]{1,0:T(8,128)(2,1)} async-done(((bf16[2048,256]{1,0:T(8,128)(2,1)}), bf16[2048,256]{1,0:T(8,128)(2,1)}) %all-reduce.5.cloned.1.call-update) | async-done | bytes 1048592 | tf_op jit(solution)/shard_map/psum | solution.py:204
  644.2 2.2 fusion.51
  (228 shorter events, 94.2 us)
Async XLA Ops:
  8.9 20.7 %all-to-all-start = ((s32[64,1,1]{2,1,0:T(1,128)}), s32[64,1,1]{2,1,0:T(1,128)S(1)}, u32[]{:S(2)}, u32[]{:S(2)}) async-start(s32[64,1,1]{2,1,0:T(1,128)} %copy.161), calls=%async_computation | async-start | bytes 65536 | tf_op jit(solution)/shard_map/all_to_all | solution.py:60
  35.2 6.7 %copy-start.8 = (s32[2]{0:T(128)S(1)}, s32[2]{0:T(128)}, u32[]{:S(2)}) copy-start(s32[2]{0:T(128)} %param.23) | copy-start | bytes 28
  35.2 18.9 %copy-start.5 = (bf16[2048,256]{1,0:T(8,128)(2,1)S(1)}, bf16[2048,256]{1,0:T(8,128)(2,1)}, u32[]{:S(2)}) copy-start(bf16[2048,256]{1,0:T(8,128)(2,1)} %param.18) | copy-start | bytes 3145732
  35.2 201.7 %all-to-all-start.1 = ((bf16[64,128,256]{2,1,0:T(8,128)(2,1)}), bf16[64,128,256]{2,1,0:T(8,128)(2,1)}, u32[]{:S(2)}, u32[]{:S(2)}) async-start(bf16[64,128,256]{2,1,0:T(8,128)(2,1)} %gather_fusion.1), calls=%async_computation.1 | async-start | bytes 8388608 | tf_op jit(solution)/shard_map/all_to_all | solution.py:64
  41.8 13.4 %copy-start.6 = (bf16[2048,256]{1,0:T(8,128)(2,1)S(1)}, bf16[2048,256]{1,0:T(8,128)(2,1)}, u32[]{:S(2)}) copy-start(bf16[2048,256]{1,0:T(8,128)(2,1)} %param.21) | copy-start | bytes 3145732
  41.8 193.1 %all-reduce.7.cloned.1.call-start = ((), (), s32[]{:S(2)}) async-start(), calls=%async_computation.5 | async-start | bytes 262144 | tf_op jit(solution)/shard_map/psum | solution.py:27
  48.4 533.9 %all-gather.3.cloned.1.call-start = ((), (), s32[]{:S(2)}) async-start(), calls=%async_computation.4 | async-start | bytes 17039360 | tf_op jit(solution)/shard_map/all_gather | solution.py:188
  48.4 187.3 %collective-permute-start = (bf16[128,256]{1,0:T(8,128)(2,1)S(1)}, bf16[128,256]{1,0:T(8,128)(2,1)S(1)}, u32[]{:S(2)}, u32[]{:S(2)}) collective-permute-start(bf16[128,256]{1,0:T(8,128)(2,1)S(1)} %get-tuple-element.429), channel_id=1, source_target_pairs={{0,4},{4,8},{8,12},{12,16},{16,20},{20,24},{24,28},{28,32},{32,36}... | collective-permute-start | bytes 196616 | tf_op jit(solution)/shard_map/ppermute | solution.py:19
  50.5 185.3 %collective-permute-start.1 = (bf16[128,256]{1,0:T(8,128)(2,1)S(1)}, bf16[128,256]{1,0:T(8,128)(2,1)S(1)}, u32[]{:S(2)}, u32[]{:S(2)}) collective-permute-start(bf16[128,256]{1,0:T(8,128)(2,1)S(1)} %get-tuple-element.430), channel_id=1, source_target_pairs={{4,0},{8,4},{12,8},{16,12},{20,16},{24,20},{28,24},{32,28},{36,32}... | collective-permute-start | bytes 196616 | tf_op jit(solution)/shard_map/ppermute | solution.py:20
  261.1 8.5 %copy-start = (f32[128,8,8,128]{3,2,1,0:T(8,128)S(1)}, f32[128,8,8,128]{3,2,1,0:T(8,128)}, u32[]{:S(2)}) copy-start(f32[128,8,8,128]{3,2,1,0:T(8,128)} %copy.241) | copy-start | bytes 12582916 | tf_op jit(solution)/shard_map/while
  271.8 1.8 copy-start.2
  273.1 1.5 copy-start.1
  274.7 6.3 copy-start.3
  303.6 9.6 %copy-start = (f32[128,8,8,128]{3,2,1,0:T(8,128)S(1)}, f32[128,8,8,128]{3,2,1,0:T(8,128)}, u32[]{:S(2)}) copy-start(f32[128,8,8,128]{3,2,1,0:T(8,128)} %copy.241) | copy-start | bytes 12582916 | tf_op jit(solution)/shard_map/while
  315.3 1.8 copy-start.2
  316.7 1.5 copy-start.1
  318.2 9.3 %copy-start.3 = (f32[18,128,256]{1,2,0:T(8,128)}, f32[18,128,256]{1,2,0:T(8,128)S(1)}, u32[]{:S(2)}) copy-start(f32[18,128,256]{1,2,0:T(8,128)S(1)} %add_dynamic-update-slice_fusion.5) | copy-start | bytes 7077892 | tf_op jit(solution)/shard_map/while
  350.2 9.6 %copy-start = (f32[128,8,8,128]{3,2,1,0:T(8,128)S(1)}, f32[128,8,8,128]{3,2,1,0:T(8,128)}, u32[]{:S(2)}) copy-start(f32[128,8,8,128]{3,2,1,0:T(8,128)} %copy.241) | copy-start | bytes 12582916 | tf_op jit(solution)/shard_map/while
  361.9 1.8 copy-start.2
  363.3 1.5 copy-start.1
  364.8 9.3 %copy-start.3 = (f32[18,128,256]{1,2,0:T(8,128)}, f32[18,128,256]{1,2,0:T(8,128)S(1)}, u32[]{:S(2)}) copy-start(f32[18,128,256]{1,2,0:T(8,128)S(1)} %add_dynamic-update-slice_fusion.5) | copy-start | bytes 7077892 | tf_op jit(solution)/shard_map/while
  396.7 9.6 %copy-start = (f32[128,8,8,128]{3,2,1,0:T(8,128)S(1)}, f32[128,8,8,128]{3,2,1,0:T(8,128)}, u32[]{:S(2)}) copy-start(f32[128,8,8,128]{3,2,1,0:T(8,128)} %copy.241) | copy-start | bytes 12582916 | tf_op jit(solution)/shard_map/while
  408.5 1.8 copy-start.2
  409.9 1.5 copy-start.1
  411.4 9.3 %copy-start.3 = (f32[18,128,256]{1,2,0:T(8,128)}, f32[18,128,256]{1,2,0:T(8,128)S(1)}, u32[]{:S(2)}) copy-start(f32[18,128,256]{1,2,0:T(8,128)S(1)} %add_dynamic-update-slice_fusion.5) | copy-start | bytes 7077892 | tf_op jit(solution)/shard_map/while
  432.3 8.4 %copy-start.9 = (s32[2]{0:T(128)S(1)}, s32[2]{0:T(128)}, u32[]{:S(2)}) copy-start(s32[2]{0:T(128)} %param.23) | copy-start | bytes 28
  432.3 8.4 %copy-start.4 = (f32[18,128,256]{1,2,0:T(8,128)S(1)}, f32[18,128,256]{1,2,0:T(8,128)}, u32[]{:S(2)}) copy-start(f32[18,128,256]{1,2,0:T(8,128)} %get-tuple-element.283) | copy-start | bytes 7077892
  432.3 136.5 %all-to-all-start.2 = ((bf16[64,128,256]{2,1,0:T(8,128)(2,1)}), bf16[64,128,256]{2,1,0:T(8,128)(2,1)}, u32[]{:S(2)}, u32[]{:S(2)}) async-start(bf16[64,128,256]{2,1,0:T(8,128)(2,1)} %copy.223), calls=%async_computation.2 | async-start | bytes 8388608 | tf_op jit(solution)/shard_map/all_to_all | solution.py:198
  440.7 203.5 %all-reduce.5.cloned.1.call-start = ((), (), s32[]{:S(2)}) async-start(), calls=%async_computation.3 | async-start | bytes 2097152 | tf_op jit(solution)/shard_map/psum | solution.py:204
  444.6 9.1 %collective-permute-start.2 = (bf16[128,256]{1,0:T(8,128)(2,1)S(1)}, bf16[128,256]{1,0:T(8,128)(2,1)S(1)}, u32[]{:S(2)}, u32[]{:S(2)}) collective-permute-start(bf16[128,256]{1,0:T(8,128)(2,1)S(1)} %get-tuple-element.424), channel_id=1, source_target_pairs={{4,0},{8,4},{12,8},{16,12},{20,16},{24,20},{28,24},{32,28},{36,32}... | collective-permute-start | bytes 196616 | tf_op jit(solution)/shard_map/ppermute | solution.py:33
  449.0 119.8 %copy-start.7 = (s32[64]{0:T(128)S(1)}, s32[64]{0:T(128)}, u32[]{:S(2)}) copy-start(s32[64]{0:T(128)} %get-tuple-element.382) | copy-start | bytes 772
  451.3 5.9 collective-permute-start.3
Sparse Core Ops, SparseCore 0:
  48.5 186.3 all-reduce.6
  422.6 159.6 all-gather.2
  593.5 50.6 all-reduce.4
